TPU v7x, 512 devices: a whole 4x8x8 slice. The times are simulated.
512 devices in a mesh: ctx: 16 (over y, core), head: 32 (over z, x).
Axes of the slice: x: 4, y: 8, z: 8, core: 2. Of those that a mesh axis runs over, the one named last changes fastest.
Arguments:
- query_rows: bfloat16 [6144, 64, 128], P('ctx', 'head'), may hold values from -1.75 to 1.75
- key_matrix: bfloat16 [6144, 64, 128], P('ctx', 'head'), may hold values from -1.75 to 1.75
- value_rows: bfloat16 [6144, 64, 128], P('ctx', 'head'), may hold values from -55 to 55
- decay_log: float32 [6144, 64], P('ctx', 'head'), may hold values from -0.6 to 0
- norm_gain: float32 [64, 128], P('head'), may hold values from 0.1 to 1.9
- grad_out: bfloat16 [6144, 64, 128], P('ctx', 'head'), may hold values from -6 to 6
Outputs:
- output: bfloat16 [6144, 64, 128], P('ctx', 'head')
- grad_query: bfloat16 [6144, 64, 128], P('ctx', 'head')
- grad_key: bfloat16 [6144, 64, 128], P('ctx', 'head')
- grad_value: bfloat16 [6144, 64, 128], P('ctx', 'head')
All inputs are finite; a program needn't handle non-finite values.
Results may differ from a plain program's by a relative error of at most 0.019.
Values sent between devices are 32-bit elements; how exact they have to be, the bound alone decides.
A program may use at most 64 MiB of HBM per device.

v0:
```python
import jax
import jax.numpy as jnp
from jax import lax
from jax.sharding import PartitionSpec as P

GROUP = 128
epsilon = 1e-06


def weigh_gathered(gathered, log_rates, position, forward):
    device_ranks = jnp.arange(log_rates.shape[0], dtype=jnp.int32)
    running = jnp.cumsum(log_rates, axis=0)
    own_total = running[position]
    if forward:
        keep_mask = device_ranks < position
        spread = (own_total - log_rates[position])[None, :] - running
    else:
        keep_mask = device_ranks > position
        spread = running - log_rates - own_total[None, :]
    keep_mask = keep_mask[:, None]
    factors = jnp.where(keep_mask, jnp.exp(jnp.where(keep_mask, spread, 0.0)), 0.0)
    return jnp.einsum("nh,nhde->hde", factors, gathered, precision=lax.Precision.HIGHEST)


def per_device(query_rows, key_matrix, value_rows, decay_log, norm_gain, grad_out):
    token_count, head_count, head_size = query_rows.shape
    num_blocks = token_count // GROUP
    query_blocks = query_rows.reshape(num_blocks, GROUP, head_count, head_size)
    key_blocks = key_matrix.reshape(num_blocks, GROUP, head_count, head_size)
    value_blocks = value_rows.reshape(num_blocks, GROUP, head_count, head_size)
    cumulative = jnp.cumsum(decay_log.reshape(num_blocks, GROUP, head_count), axis=1)
    block_total = cumulative[:, -1, :]
    cum_major = jnp.transpose(cumulative, (0, 2, 1))
    row_ids = lax.broadcasted_iota(jnp.int32, (GROUP, GROUP), 0)
    col_ids = lax.broadcasted_iota(jnp.int32, (GROUP, GROUP), 1)
    causal = (row_ids >= col_ids)[None, None]
    spread = cum_major[:, :, :, None] - cum_major[:, :, None, :]
    mask_weight = jnp.where(causal, jnp.exp(jnp.where(causal, spread, 0.0)), 0.0)
    scores = jnp.einsum(
        "cihd,cjhd->chij", query_blocks, key_blocks, preferred_element_type=jnp.float32
    )
    attn_weights = (scores * mask_weight).astype(jnp.bfloat16)
    local_part = jnp.einsum(
        "chij,cjhd->cihd", attn_weights, value_blocks, preferred_element_type=jnp.float32
    )

    def advance(carry_state, pieces):
        key_part, value_part, cum_part, total_part = pieces
        decayed = (key_part * jnp.exp(total_part[None, :] - cum_part)[:, :, None]).astype(
            jnp.bfloat16
        )
        fresh_term = jnp.einsum(
            "ihd,ihe->hde", decayed, value_part, preferred_element_type=jnp.float32
        )
        return (jnp.exp(total_part)[:, None, None] * carry_state + fresh_term, carry_state)

    zero_state = jnp.zeros((head_count, head_size, head_size), jnp.float32)
    end_state, local_states = lax.scan(
        advance, zero_state, (key_blocks, value_blocks, cumulative, block_total)
    )
    total_log = jnp.sum(block_total, axis=0)
    position = lax.axis_index("ctx")
    gathered, log_rates = (
        lax.all_gather(end_state[None], "ctx", axis=0, tiled=True),
        lax.all_gather(total_log[None], "ctx", axis=0, tiled=True),
    )
    incoming = weigh_gathered(gathered, log_rates, position, True)
    before = jnp.cumsum(block_total, axis=0) - block_total
    state_bf = (local_states + jnp.exp(before)[:, :, None, None] * incoming[None]).astype(
        jnp.bfloat16
    )
    carried_part = (
        jnp.einsum("cihd,chde->cihe", query_blocks, state_bf, preferred_element_type=jnp.float32)
        * jnp.exp(cumulative)[:, :, :, None]
    )
    attention = (
        (local_part + carried_part).astype(jnp.bfloat16).reshape(token_count, head_count, head_size)
    )
    attn_f = attention.astype(jnp.float32)
    grad_f = grad_out.astype(jnp.float32)
    features = head_count * lax.axis_size("head") * head_size
    square_sum = lax.psum(jnp.sum(attn_f * attn_f, axis=(1, 2)), "head")
    inv_rms = lax.rsqrt(square_sum / features + epsilon)
    output = (attn_f * inv_rms[:, None, None] * norm_gain[None]).astype(jnp.bfloat16)
    scaled_grad = norm_gain[None] * (grad_f + output.astype(jnp.float32))
    inner = lax.psum(jnp.sum(scaled_grad * attn_f, axis=(1, 2)), "head")
    grad_attention = (
        inv_rms[:, None, None] * scaled_grad
        - attn_f * (inv_rms**3 * inner / features)[:, None, None]
    ).astype(jnp.bfloat16)
    grad_blocks = grad_attention.reshape(num_blocks, GROUP, head_count, head_size)
    grad_dots = jnp.einsum(
        "cihe,cjhe->chij", grad_blocks, value_blocks, preferred_element_type=jnp.float32
    )
    grad_scores = (grad_dots * mask_weight).astype(jnp.bfloat16)
    query_local = jnp.einsum(
        "chij,cjhd->cihd", grad_scores, key_blocks, preferred_element_type=jnp.float32
    )
    key_local = jnp.einsum(
        "chij,cihd->cjhd", grad_scores, query_blocks, preferred_element_type=jnp.float32
    )
    value_local = jnp.einsum(
        "chij,cihe->cjhe", attn_weights, grad_blocks, preferred_element_type=jnp.float32
    )
    query_carried = (
        jnp.einsum("cihe,chde->cihd", grad_blocks, state_bf, preferred_element_type=jnp.float32)
        * jnp.exp(cumulative)[:, :, :, None]
    )

    def retreat(carry_state, pieces):
        query_part, grad_part, cum_part, total_part = pieces
        decayed = (query_part * jnp.exp(cum_part)[:, :, None]).astype(jnp.bfloat16)
        fresh_term = jnp.einsum(
            "ihd,ihe->hde", decayed, grad_part, preferred_element_type=jnp.float32
        )
        return (jnp.exp(total_part)[:, None, None] * carry_state + fresh_term, carry_state)

    start_state, local_back = lax.scan(
        retreat, zero_state, (query_blocks, grad_blocks, cumulative, block_total), reverse=True
    )
    gathered_back, log_back = (
        lax.all_gather(start_state[None], "ctx", axis=0, tiled=True),
        lax.all_gather(total_log[None], "ctx", axis=0, tiled=True),
    )
    arriving = weigh_gathered(gathered_back, log_back, position, False)
    after = total_log[None, :] - jnp.cumsum(block_total, axis=0)
    back_bf = (local_back + jnp.exp(after)[:, :, None, None] * arriving[None]).astype(jnp.bfloat16)
    tail = jnp.exp(block_total[:, None, :] - cumulative)[:, :, :, None]
    key_carried = (
        jnp.einsum("cihe,chde->cihd", value_blocks, back_bf, preferred_element_type=jnp.float32)
        * tail
    )
    value_carried = (
        jnp.einsum("cihd,chde->cihe", key_blocks, back_bf, preferred_element_type=jnp.float32)
        * tail
    )
    shape_out = (token_count, head_count, head_size)
    grad_query = (query_local + query_carried).astype(jnp.bfloat16).reshape(shape_out)
    grad_key = (key_local + key_carried).astype(jnp.bfloat16).reshape(shape_out)
    grad_value = (value_local + value_carried).astype(jnp.bfloat16).reshape(shape_out)
    return (output, grad_query, grad_key, grad_value)


def solution(mesh):
    placed = (
        P("ctx", "head", None),
        P("ctx", "head", None),
        P("ctx", "head", None),
        P("ctx", "head"),
        P("head", None),
        P("ctx", "head", None),
    )
    return jax.shard_map(
        per_device,
        mesh=mesh,
        in_specs=placed,
        out_specs=(
            P("ctx", "head", None),
            P("ctx", "head", None),
            P("ctx", "head", None),
            P("ctx", "head", None),
        ),
        check_vma=False,
    )
```

profile of v0, /device:TPU:1, one launch (start us, length us, event | category | flops | bytes accessed | tf_op | source)
XLA Modules:
  0.0 262.6 jit_solution(10493295506692607835)
XLA Ops:
  7.2 0.8 copy.129
  8.6 1.0 copy.79
  9.5 1.0 copy.85
  10.6 1.4 while.30
  12.0 0.6 copy-done.1
  12.9 1.3 dynamic-slice
  15.1 29.7 %all-reduce = f32[32]{0:T(128)S(1)} all-reduce(f32[32]{0:T(128)S(1)} %dynamic-update-slice), channel_id=2, replica_groups=mesh['ctx'=16,'head'=32] {'ctx'}, use_global_device_ids=true, to_apply=%add | all-reduce | flops 32 | bytes 256
  45.9 14.7 %all-gather.6.cloned.1.call-done = f32[32,128,128]{2,1,0:T(8,128)} async-done(((f32[2,128,128]{2,1,0:T(8,128)}), f32[32,128,128]{2,1,0:T(8,128)}) %all-gather.6.cloned.1.call-update) | async-done | bytes 2097168 | tf_op jit(solution)/shard_map/all_gather | solution.py:64
  60.6 3.8 %fusion.24 = f32[2,1,128,128]{3,1,2,0:T(1,128)S(1)} fusion(f32[16,2,1,1]{0,2,3,1:T(1,128)S(1)} %copy.121, f32[16,2,128,128]{3,2,1,0:T(8,128)} %bitcast.159), kind=kOutput, calls=%fused_computation.34 | convolution fusion | flops 6291456 | bytes 2228352 | tf_op jit(solution)/shard_map/nh,nhde->hde/dot_general | solution.py:22
  64.4 0.3 fusion.27
  64.6 0.3 multiply_reduce_fusion
  65.0 61.6 %psum.14 = f32[384]{0:T(512)S(1)} all-reduce(f32[384]{0:T(512)S(1)} %bitcast.171), channel_id=1, replica_groups=mesh['ctx'=16,'head'=32] {'head'}, use_global_device_ids=true, to_apply=%region_7.8 | all-reduce | flops 384 | bytes 3072 | tf_op jit(solution)/shard_map/psum | solution.py:82
  126.9 56.2 %psum.15 = f32[384]{0:T(512)S(1)} all-reduce(f32[384]{0:T(512)S(1)} %fusion.43), channel_id=1, replica_groups=mesh['ctx'=16,'head'=32] {'head'}, use_global_device_ids=true, to_apply=%region_9.10 | all-reduce | flops 384 | bytes 3072 | tf_op jit(solution)/shard_map/psum | solution.py:86
  183.4 1.2 while.31
  184.6 0.6 copy-done
  185.6 0.9 copy.117
  186.7 0.3 fusion.31
  187.3 0.9 copy.118
  188.2 60.8 %all-gather.8.cloned.1.call-done = f32[32,128,128]{2,1,0:T(8,128)} async-done(((f32[2,128,128]{2,1,0:T(8,128)}), f32[32,128,128]{2,1,0:T(8,128)}) %all-gather.8.cloned.1.call-update) | async-done | bytes 2097168 | tf_op jit(solution)/shard_map/all_gather | solution.py:122
  249.0 3.8 %fusion.22 = f32[2,1,128,128]{3,1,2,0:T(1,128)S(1)} fusion(f32[16,2,1,1]{0,2,3,1:T(1,128)S(1)} %copy.125, f32[16,2,128,128]{3,2,1,0:T(8,128)} %bitcast.160), kind=kOutput, calls=%fused_computation.32 | convolution fusion | flops 6291456 | bytes 2228352 | tf_op jit(solution)/shard_map/nh,nhde->hde/dot_general | solution.py:22
  252.8 0.3 fusion.29
  253.1 0.3 fusion.26
  253.7 0.9 copy.119
  254.9 0.9 copy.120
  (91 shorter events, 6.3 us)
Async XLA Ops:
  7.2 53.4 %all-gather.6.cloned.1.call-start = ((), (), s32[]{:S(2)}) async-start(), calls=%async_computation | async-start | bytes 2228224 | tf_op jit(solution)/shard_map/all_gather | solution.py:64
  10.6 2.3 copy-start.3
  12.0 0.7 copy-start.1
  12.6 236.4 %all-gather.8.cloned.1.call-start = ((), (), s32[]{:S(2)}) async-start(), calls=%async_computation.1 | async-start | bytes 2228224 | tf_op jit(solution)/shard_map/all_gather | solution.py:122
  64.3 62.3 %copy-start.2 = (bf16[384,2,128]{2,1,0:T(2,128)(2,1)S(1)}, bf16[384,2,128]{2,1,0:T(2,128)(2,1)}, u32[]{:S(2)}) copy-start(bf16[384,2,128]{2,1,0:T(2,128)(2,1)} %param.15) | copy-start | bytes 589828
  64.4 62.3 %copy-start.4 = (f32[2,128]{1,0:T(2,128)S(1)}, f32[2,128]{1,0:T(2,128)}, u32[]{:S(2)}) copy-start(f32[2,128]{1,0:T(2,128)} %param.14) | copy-start | bytes 3076
  184.6 0.7 copy-start
Sparse Core Ops, SparseCore 0:
  12.8 47.7 all-gather.5
  185.4 63.5 all-gather.7
where the time goes:
time: 263 us
  blocking collectives  148 us (56%)
  waiting for transfers between devices  75.5 us (29%)
  between operations  15 us (6%)
  matrix products  11.3 us (4%)
  local copies, waits for them, and re-layouts  11.2 us (4%)
    psum x1, blocking collectives, per_device(): square_sum = lax.psum(jnp.sum(attn_f * attn_f, axis=(1, 2)), 'head')  61.6 us
    all_gather x1, waiting for transfers between devices, per_device(): lax.all_gather(start_state[None], 'ctx', axis=0, tiled=True)  60.8 us
    psum x1, blocking collectives, per_device(): inner = lax.psum(jnp.sum(scaled_grad * attn_f, axis=(1, 2)), 'head')  56.2 us
    unnamed x1, blocking collectives  29.7 us
    all_gather x1, waiting for transfers between devices, per_device(): lax.all_gather(end_state[None], 'ctx', axis=0, tiled=True)  14.7 us
    unnamed x22, local copies, waits for them, and re-layouts  8.56 us
    dot_general x2, matrix products, weigh_gathered(): jnp.einsum('nh,nhde->hde', factors, gathered, precision=lax.Precision.HIG...  7.53 us
  transfers between devices with their start and end apart: 2, of which 2 were waited for; matrix products, arithmetic and copies ran while one was open for 2% of the time, Pallas kernels for 0%

commit v1 on v0

--- a/solution.py
+++ b/solution.py
@@ -61,7 +61,9 @@
     total_log = jnp.sum(block_total, axis=0)
     position = lax.axis_index("ctx")
     gathered, log_rates = (
-        lax.all_gather(end_state[None], "ctx", axis=0, tiled=True),
+        jnp.concatenate(
+            lax.all_to_all(jnp.stack([end_state[None]] * lax.axis_size("ctx")), "ctx", 0, 0), axis=0
+        ),
         lax.all_gather(total_log[None], "ctx", axis=0, tiled=True),
     )
     incoming = weigh_gathered(gathered, log_rates, position, True)

time: 263 us -> 305 us (1.16)
  blocking collectives: 148 us -> 185 us
  waiting for transfers between devices: 75.5 us -> 62.2 us
  starting transfers between devices: 0.08 us -> 10.5 us
  local copies, waits for them, and re-layouts: 11.2 us -> 16.6 us
    unnamed x1, blocking collectives: 29.7 us -> 63.9 us
    all_gather x1 -> x0, waiting for transfers between devices: 14.7 us -> none  [per_device(): lax.all_gather(end_state[None], 'ctx', axis=0, tiled=True)]
    all_to_all x0 -> x1, starting transfers between devices: none -> 10.5 us  [per_device(): lax.all_to_all(jnp.stack([end_state[None]] * lax.axis_size('ctx')), 'ctx'...]
    psum x1, blocking collectives: 61.6 us -> 65.3 us  [per_device(): square_sum = lax.psum(jnp.sum(attn_f * attn_f, axis=(1, 2)), 'head')]
    unnamed x22 -> x44, local copies, waits for them, and re-layouts: 8.56 us -> 9.16 us
  transfers between devices with their start and end apart: 2 -> 2, of which waited for: 2 -> 1; matrix products, arithmetic and copies ran while one was open for 2% -> 3% of each run, Pallas kernels for 0% -> 0%
where the time goes in v1:
time: 305 us
  blocking collectives  185 us (61%)
  waiting for transfers between devices  62.2 us (20%)
  local copies, waits for them, and re-layouts  16.6 us (5%)
  between operations  15.1 us (5%)
  matrix products  11.2 us (4%)
  starting transfers between devices  10.5 us (3%)
  other arithmetic  3.37 us (1%)
    psum x1, blocking collectives, per_device(): square_sum = lax.psum(jnp.sum(attn_f * attn_f, axis=(1, 2)), 'head')  65.3 us
    unnamed x1, blocking collectives  63.9 us
    all_gather x1, waiting for transfers between devices, per_device(): lax.all_gather(start_state[None], 'ctx', axis=0, tiled=True)  62.2 us
    psum x1, blocking collectives, per_device(): inner = lax.psum(jnp.sum(scaled_grad * attn_f, axis=(1, 2)), 'head')  56.1 us
    all_to_all x1, starting transfers between devices, per_device(): lax.all_to_all(jnp.stack([end_state[None]] * lax.axis_size('ctx')), 'ctx'...  10.5 us
    unnamed x44, local copies, waits for them, and re-layouts  9.16 us
    dot_general x2, matrix products, weigh_gathered(): jnp.einsum('nh,nhde->hde', factors, gathered, precision=lax.Precision.HIG...  6.7 us
  transfers between devices with their start and end apart: 2, of which 1 were waited for; matrix products, arithmetic and copies ran while one was open for 3% of the time, Pallas kernels for 0%

profile of v1, /device:TPU:1, one launch (start us, length us, event | category | flops | bytes accessed | tf_op | source)
XLA Modules:
  0.0 304.6 jit_solution(9493013690401350437)
XLA Ops:
  7.2 0.8 copy.129
  8.5 1.0 copy.85
  9.5 1.0 copy.79
  10.5 1.4 while.30
  11.9 1.6 stack.3
  13.5 10.5 %all-to-all-start = ((f32[16,1,2,128,128]{4,3,2,1,0:T(8,128)}), f32[16,1,2,128,128]{4,3,2,1,0:T(8,128)S(1)}, u32[]{:S(2)}, u32[]{:S(2)}) async-start(f32[16,1,2,128,128]{4,3,2,1,0:T(8,128)} %stack.3), calls=%async_computation | async-start | bytes 4194304 | tf_op jit(solution)/shard_map/all_to_all | solution.py:65
  24.0 1.3 dynamic-slice
  26.2 63.9 %all-reduce = f32[32]{0:T(128)S(1)} all-reduce(f32[32]{0:T(128)S(1)} %dynamic-update-slice), channel_id=2, replica_groups=mesh['ctx'=16,'head'=32] {'ctx'}, use_global_device_ids=true, to_apply=%add | all-reduce | flops 32 | bytes 256
  91.2 1.3 subtract_exponential_fusion.1
  93.1 0.7 subtract_exponential_fusion
  93.9 1.0 copy.78
  95.7 2.9 fusion.24
  98.6 1.0 fusion.27
  99.9 65.3 %psum.14 = f32[384]{0:T(512)S(1)} all-reduce(f32[384]{0:T(512)S(1)} %bitcast.171), channel_id=1, replica_groups=mesh['ctx'=16,'head'=32] {'head'}, use_global_device_ids=true, to_apply=%region_7.8 | all-reduce | flops 384 | bytes 3072 | tf_op jit(solution)/shard_map/psum | solution.py:84
  165.4 56.1 %psum.15 = f32[384]{0:T(512)S(1)} all-reduce(f32[384]{0:T(512)S(1)} %fusion.43), channel_id=1, replica_groups=mesh['ctx'=16,'head'=32] {'head'}, use_global_device_ids=true, to_apply=%region_9.10 | all-reduce | flops 384 | bytes 3072 | tf_op jit(solution)/shard_map/psum | solution.py:88
  221.9 3.3 %while.31 = (s32[]{:T(128)}, f32[2,128,128]{2,1,0:T(8,128)S(1)}, f32[3,2,128,128]{3,2,1,0:T(8,128)S(1)}, f32[3,2]{1,0:T(4,128)}, bf16[3,128,2,128]{3,1,0,2:T(8,1...) while((s32[]{:T(128)}, f32[2,128,128]{2,1,0:T(8,128)S(1)}, ...), condition=%wide.region_11.12_spmd.clone, body=%wide.region_10.11_spmd.clone.sunk | while | flops 8617988 | bytes 921248 | solution.py:120
  222.1 0.7 fusion.84
  224.3 0.7 fusion.84
  227.0 0.9 copy.118
  227.9 0.9 copy.117
  228.7 62.2 %all-gather.4.cloned.1.call-done = f32[32,128,128]{2,1,0:T(8,128)} async-done(((f32[2,128,128]{2,1,0:T(8,128)}), f32[32,128,128]{2,1,0:T(8,128)}) %all-gather.4.cloned.1.call-update) | async-done | bytes 2097168 | tf_op jit(solution)/shard_map/all_gather | solution.py:124
  291.0 3.8 %fusion.22 = f32[2,1,128,128]{3,1,2,0:T(1,128)S(1)} fusion(f32[16,2,1,1]{0,2,3,1:T(1,128)S(1)} %copy.125, f32[16,2,128,128]{3,2,1,0:T(8,128)} %bitcast.160), kind=kOutput, calls=%fused_computation.32 | convolution fusion | flops 6291456 | bytes 2228352 | tf_op jit(solution)/shard_map/nh,nhde->hde/dot_general | solution.py:22
  295.7 0.9 copy.120
  296.9 0.9 copy.119
  (113 shorter events, 10.1 us)
Async XLA Ops:
  8.2 17.7 %copy-start.15 = (f32[2]{0:T(128)}, f32[2]{0:T(128)S(1)}, u32[]{:S(2)}) copy-start(f32[2]{0:T(128)S(1)} %get-tuple-element.320) | copy-start | bytes 28
  8.4 2.1 copy-start.9
  11.9 81.2 %copy-start.5 = (f32[3,2]{1,0:T(4,128)}, f32[3,2]{1,0:T(4,128)S(1)}, u32[]{:S(2)}) copy-start(f32[3,2]{1,0:T(4,128)S(1)} %get-tuple-element.489) | copy-start | bytes 76
  13.5 77.5 %copy-start.10 = (f32[3,1,2]{0,2,1:T(2,128)S(1)}, f32[3,1,2]{0,2,1:T(2,128)}, u32[]{:S(2)}) copy-start(f32[3,1,2]{0,2,1:T(2,128)} %copy-done.9) | copy-start | bytes 76
  13.5 81.9 %all-to-all-start = ((f32[16,1,2,128,128]{4,3,2,1,0:T(8,128)}), f32[16,1,2,128,128]{4,3,2,1,0:T(8,128)S(1)}, u32[]{:S(2)}, u32[]{:S(2)}) async-start(f32[16,1,2,128,128]{4,3,2,1,0:T(8,128)} %stack.3), calls=%async_computation | async-start | bytes 4194304 | tf_op jit(solution)/shard_map/all_to_all | solution.py:65
  24.0 267.0 %all-gather.4.cloned.1.call-start = ((), (), s32[]{:S(2)}) async-start(), calls=%async_computation.1 | async-start | bytes 2228224 | tf_op jit(solution)/shard_map/all_gather | solution.py:124
  95.0 0.6 copy-start.13
  95.0 0.6 copy-start.7
  95.3 4.6 %copy-start.3 = (bf16[3,2,128,128]{3,2,1,0:T(8,128)(2,1)}, bf16[3,2,128,128]{3,2,1,0:T(8,128)(2,1)S(1)}, u32[]{:S(2)}) copy-start(bf16[3,2,128,128]{3,2,1,0:T(8,128)(2,1)S(1)} %fusion.34) | copy-start | bytes 589828
  98.6 66.6 %copy-start.2 = (bf16[384,2,128]{2,1,0:T(2,128)(2,1)S(1)}, bf16[384,2,128]{2,1,0:T(2,128)(2,1)}, u32[]{:S(2)}) copy-start(bf16[384,2,128]{2,1,0:T(2,128)(2,1)} %param.15) | copy-start | bytes 589828
  98.6 66.6 %copy-start.11 = (f32[2,128]{1,0:T(2,128)S(1)}, f32[2,128]{1,0:T(2,128)}, u32[]{:S(2)}) copy-start(f32[2,128]{1,0:T(2,128)} %param.14) | copy-start | bytes 3076
  221.8 4.1 %copy-start.12 = (f32[3,2]{0,1:T(2,128)S(1)}, f32[3,2]{0,1:T(2,128)}, u32[]{:S(2)}) copy-start(f32[3,2]{0,1:T(2,128)} %get-tuple-element.326) | copy-start | bytes 76
  221.8 4.2 %copy-start.1 = (f32[3,128,2]{2,1,0:T(8,128)S(1)}, f32[3,128,2]{2,1,0:T(8,128)}, u32[]{:S(2)}) copy-start(f32[3,128,2]{2,1,0:T(8,128)} %get-tuple-element.318) | copy-start | bytes 9220
  221.9 4.2 %copy-start.8 = (pred[128,128]{1,0:T(8,128)(4,1)S(1)}, pred[128,128]{1,0:T(8,128)(4,1)}, u32[]{:S(2)}) copy-start(pred[128,128]{1,0:T(8,128)(4,1)} %copy-done.7) | copy-start | bytes 49156
  221.9 4.2 %copy-start.14 = (f32[3,2,128]{2,1,0:T(2,128)S(1)}, f32[3,2,128]{2,1,0:T(2,128)}, u32[]{:S(2)}) copy-start(f32[3,2,128]{2,1,0:T(2,128)} %copy-done.13) | copy-start | bytes 9220
  221.9 4.5 %copy-start.6 = (f32[3,2]{1,0:T(4,128)S(1)}, f32[3,2]{1,0:T(4,128)}, u32[]{:S(2)}) copy-start(f32[3,2]{1,0:T(4,128)} %copy.92) | copy-start | bytes 76
  225.2 0.7 copy-start
  291.0 4.4 %copy-start.4 = (bf16[3,2,128,128]{3,2,1,0:T(8,128)(2,1)S(1)}, bf16[3,2,128,128]{3,2,1,0:T(8,128)(2,1)}, u32[]{:S(2)}) copy-start(bf16[3,2,128,128]{3,2,1,0:T(8,128)(2,1)} %copy-done.3) | copy-start | bytes 589828
Sparse Core Ops, SparseCore 0:
  226.0 64.9 all-gather.3

commit v2 on v0

--- a/solution.py
+++ b/solution.py
@@ -83,7 +83,7 @@
     inv_rms = lax.rsqrt(square_sum / features + epsilon)
     output = (attn_f * inv_rms[:, None, None] * norm_gain[None]).astype(jnp.bfloat16)
     scaled_grad = norm_gain[None] * (grad_f + output.astype(jnp.float32))
-    inner = lax.psum(jnp.sum(scaled_grad * attn_f, axis=(1, 2)), "head")
+    inner = jnp.sum(lax.all_gather(jnp.sum(scaled_grad * attn_f, axis=(1, 2)), "head"), axis=0)
     grad_attention = (
         inv_rms[:, None, None] * scaled_grad
         - attn_f * (inv_rms**3 * inner / features)[:, None, None]

time: 263 us -> 239 us (0.909)
  blocking collectives: 148 us -> 123 us
    psum x1 -> x0, blocking collectives: 56.2 us -> none  [per_device(): inner = lax.psum(jnp.sum(scaled_grad * attn_f, axis=(1, 2)), 'head')]
    all_gather x0 -> x1, blocking collectives: none -> 31.7 us  [per_device(): lax.all_gather(jnp.sum(scaled_grad * attn_f, axis=(1, 2)), 'head')]
    unnamed x22 -> x23, local copies, waits for them, and re-layouts: 8.56 us -> 8.57 us
where the time goes in v2:
time: 239 us; the launch traced here: 238 us
  blocking collectives  123 us (51%)
  waiting for transfers between devices  75.9 us (32%)
  between operations  15 us (6%)
  matrix products  11.3 us (5%)
  local copies, waits for them, and re-layouts  11.2 us (5%)
    psum x1, blocking collectives, per_device(): square_sum = lax.psum(jnp.sum(attn_f * attn_f, axis=(1, 2)), 'head')  61.6 us
    all_gather x1, waiting for transfers between devices, per_device(): lax.all_gather(start_state[None], 'ctx', axis=0, tiled=True)  61.2 us
    all_gather x1, blocking collectives, per_device(): lax.all_gather(jnp.sum(scaled_grad * attn_f, axis=(1, 2)), 'head')  31.7 us
    unnamed x1, blocking collectives  29.7 us
    all_gather x1, waiting for transfers between devices, per_device(): lax.all_gather(end_state[None], 'ctx', axis=0, tiled=True)  14.7 us
    unnamed x23, local copies, waits for them, and re-layouts  8.57 us
    dot_general x2, matrix products, weigh_gathered(): jnp.einsum('nh,nhde->hde', factors, gathered, precision=lax.Precision.HIG...  7.53 us
  transfers between devices with their start and end apart: 2, of which 2 were waited for; matrix products, arithmetic and copies ran while one was open for 2% of the time, Pallas kernels for 0%

profile of v2, /device:TPU:1, one launch (start us, length us, event | category | flops | bytes accessed | tf_op | source)
XLA Modules:
  0.0 238.5 jit_solution(4066593170136700170)
XLA Ops:
  7.2 0.8 copy.129
  8.6 1.0 copy.79
  9.5 1.0 copy.85
  10.6 1.4 while.30
  12.0 0.6 copy-done.1
  12.9 1.3 dynamic-slice
  15.1 29.7 %all-reduce = f32[32]{0:T(128)S(1)} all-reduce(f32[32]{0:T(128)S(1)} %dynamic-update-slice), channel_id=2, replica_groups=mesh['ctx'=16,'head'=32] {'ctx'}, use_global_device_ids=true, to_apply=%add | all-reduce | flops 32 | bytes 256
  45.9 14.7 %all-gather.8.cloned.1.call-done = f32[32,128,128]{2,1,0:T(8,128)} async-done(((f32[2,128,128]{2,1,0:T(8,128)}), f32[32,128,128]{2,1,0:T(8,128)}) %all-gather.8.cloned.1.call-update) | async-done | bytes 2097168 | tf_op jit(solution)/shard_map/all_gather | solution.py:64
  60.6 3.8 %fusion.24 = f32[2,1,128,128]{3,1,2,0:T(1,128)S(1)} fusion(f32[16,2,1,1]{0,2,3,1:T(1,128)S(1)} %copy.121, f32[16,2,128,128]{3,2,1,0:T(8,128)} %bitcast.159), kind=kOutput, calls=%fused_computation.34 | convolution fusion | flops 6291456 | bytes 2228352 | tf_op jit(solution)/shard_map/nh,nhde->hde/dot_general | solution.py:22
  64.4 0.3 fusion.27
  64.6 0.3 multiply_reduce_fusion
  65.0 61.6 %psum.7 = f32[384]{0:T(512)S(1)} all-reduce(f32[384]{0:T(512)S(1)} %bitcast.171), channel_id=1, replica_groups=mesh['ctx'=16,'head'=32] {'head'}, use_global_device_ids=true, to_apply=%region_7.8 | all-reduce | flops 384 | bytes 3072 | tf_op jit(solution)/shard_map/psum | solution.py:82
  126.9 31.7 %all-gather.4 = f32[32,1,384]{2,1,0:T(1,128)S(1)} all-gather(f32[1,1,384]{2,1,0:T(1,128)S(1)} %reshape.158), channel_id=4, replica_groups=mesh['ctx'=16,'head'=32] {'head'}, dimensions={0}, use_global_device_ids=true | all-gather | bytes 50688 | tf_op jit(solution)/shard_map/all_gather | solution.py:86
  158.9 1.2 while.31
  160.1 0.6 copy-done
  161.1 0.9 copy.117
  162.2 0.3 fusion.31
  162.8 0.9 copy.118
  163.7 61.2 %all-gather.10.cloned.1.call-done = f32[32,128,128]{2,1,0:T(8,128)} async-done(((f32[2,128,128]{2,1,0:T(8,128)}), f32[32,128,128]{2,1,0:T(8,128)}) %all-gather.10.cloned.1.call-update) | async-done | bytes 2097168 | tf_op jit(solution)/shard_map/all_gather | solution.py:122
  224.9 3.8 %fusion.22 = f32[2,1,128,128]{3,1,2,0:T(1,128)S(1)} fusion(f32[16,2,1,1]{0,2,3,1:T(1,128)S(1)} %copy.125, f32[16,2,128,128]{3,2,1,0:T(8,128)} %bitcast.160), kind=kOutput, calls=%fused_computation.32 | convolution fusion | flops 6291456 | bytes 2228352 | tf_op jit(solution)/shard_map/nh,nhde->hde/dot_general | solution.py:22
  228.7 0.3 fusion.29
  229.0 0.3 fusion.26
  229.6 0.9 copy.119
  230.8 0.9 copy.120
  (93 shorter events, 6.3 us)
Async XLA Ops:
  7.2 53.4 %all-gather.8.cloned.1.call-start = ((), (), s32[]{:S(2)}) async-start(), calls=%async_computation | async-start | bytes 2228224 | tf_op jit(solution)/shard_map/all_gather | solution.py:64
  10.6 2.3 copy-start.3
  12.0 0.7 copy-start.1
  12.6 212.3 %all-gather.10.cloned.1.call-start = ((), (), s32[]{:S(2)}) async-start(), calls=%async_computation.1 | async-start | bytes 2228224 | tf_op jit(solution)/shard_map/all_gather | solution.py:122
  64.3 62.3 %copy-start.2 = (bf16[384,2,128]{2,1,0:T(2,128)(2,1)S(1)}, bf16[384,2,128]{2,1,0:T(2,128)(2,1)}, u32[]{:S(2)}) copy-start(bf16[384,2,128]{2,1,0:T(2,128)(2,1)} %param.15) | copy-start | bytes 589828
  64.4 62.3 %copy-start.4 = (f32[2,128]{1,0:T(2,128)S(1)}, f32[2,128]{1,0:T(2,128)}, u32[]{:S(2)}) copy-start(f32[2,128]{1,0:T(2,128)} %param.14) | copy-start | bytes 3076
  160.1 0.7 copy-start
Sparse Core Ops, SparseCore 0:
  12.8 47.7 all-gather.7
  160.9 63.9 all-gather.9
